TPU v7x, 256 devices: a whole 4x4x8 slice. The times are simulated.
256 devices in a mesh: src: 16 (over y_lo, z), tgt: 16 (over x, y_hi, core).
Axes of the slice: x: 4, y: 4 (y_hi: 2, y_lo: 2; y = y_hi * 2 + y_lo), z: 8, core: 2. Of those that a mesh axis runs over, the one named last changes fastest.
Arguments:
- coefficients: float32 [2048, 128, 512], P(('src', 'tgt')), may hold values from -6 to 6
- transfer: float32 [8, 2048, 128, 256], P(None, ('src', 'tgt')), may hold values from -0.375 to 0.375
- local_bits: int32 [4], replicated, may hold values from 0 to 2
- relabel: int32 [1024], replicated, may hold values from 0 to 1023, each once
Outputs:
- result: float32 [2048, 128, 512], P(('src', 'tgt'))
Inputs may be any that keep to these rules, and one draw needn't show every extreme that they name: `local_bits`: each entry names a bit of a node's position among the 8 nodes of one device. `relabel`: a permutation of the 1024 rows of one device.
All inputs are finite; a program needn't handle non-finite values.
Results may differ from a plain program's by a relative error of at most 0.00007.
Values sent between devices are 32-bit elements; how exact they have to be, the bound alone decides.
A program may use at most 64 MiB of HBM per device.

v0:
```python
import jax
import jax.numpy as jnp
from jax import lax
from jax.experimental import pallas as pl
from jax.experimental.pallas import tpu as pltpu
from jax.sharding import PartitionSpec as P

MESH = pl.DeviceIdType.MESH
F32 = jnp.float32
BF16 = jnp.bfloat16
CHUNKS = 4
WIDTH = 128
RANK = 128
NODES = 8
HALF = 4


def flip(index, mask):
    for bit in (1, 2, 4, 8):
        if mask & bit:
            index = index + bit - 2 * bit * (lax.div(index, bit) % 2)
    return index


def pick(bit, options):
    return jnp.where(bit == 0, options[0], jnp.where(bit == 1, options[1], options[2]))


def bits_of(number):
    return (number >> 2) & 1, (number >> 1) & 1, number & 1


def slot_node(slot, bit):
    a, b, e = bits_of(slot)
    return pick(bit, (4 * a + 2 * b + e, 4 * a + 2 * e + b, 4 * e + 2 * a + b))


def node_slot(node, bit):
    c, b, a = bits_of(node)
    return pick(bit, (4 * c + 2 * b + a, 4 * c + 2 * a + b, 4 * b + 2 * a + c))


def lower(node, bit):
    return pick(bit, (node & ~1, node & ~2, node & ~4))


def upper(node, bit):
    return pick(bit, (node | 1, node | 2, node | 4))


def split(value):
    high = value.astype(BF16)
    low = (value - high.astype(F32)).astype(BF16)
    return jnp.concatenate([high, low], axis=1)


def product(block, state):
    full = jnp.dot(block, state, preferred_element_type=F32)
    both = full[:, :WIDTH] + full[:, WIDTH:]
    return [both[r : r + RANK] + both[r + RANK : r + 2 * RANK] for r in range(0, both.shape[0], 2 * RANK)]


def stack(first, second):
    return jnp.concatenate([first, second], axis=0)


def kernel(
    bits, relabel, coef_hbm, g_hbm, out_hbm,
    x0, graw0, graw, gpart, gb, xa, xc, xe, xf, onehot,
    s0, r1, s2, r3, pm, mid, t4, s4, s5, r6, out,
    tab, in_sem, gs_sem, gr_sem,
    send1, recv1, send3, recv3, sendm, recvm, send4, recv4, send6, recv6, out_sem,
):
    src = lax.axis_index("src")
    tgt = lax.axis_index("tgt")
    far = lax.div(tgt, 8)
    near = tgt % 8
    peer1 = (flip(src, 8), tgt)
    peer3 = (flip(src, 1), tgt)
    peer4 = (src, flip(tgt, 8))
    peer6 = (src, flip(tgt, 1))
    side1 = lax.div(src, 8)
    side3 = src % 2
    side6 = tgt % 2

    barrier = pltpu.get_barrier_semaphore()
    peers = [peer1, peer3, peer4] + [(src, flip(tgt, i)) for i in range(1, 8)]
    for peer in peers:
        pl.semaphore_signal(barrier, inc=1, device_id=peer, device_id_type=MESH)

    load_x = pltpu.make_async_copy(coef_hbm, x0, in_sem.at[0])
    load_g0 = pltpu.make_async_copy(g_hbm.at[0], graw0, in_sem.at[1])
    load_g = pltpu.make_async_copy(g_hbm.at[pl.ds(1, 7)], graw, in_sem.at[2])
    load_g0.start()
    load_x.start()
    load_g.start()

    b0, b1, b2, b3 = bits[0], bits[1], bits[2], bits[3]
    for n in range(NODES):
        nu = slot_node(n, b1)
        tab[0, n] = nu
        tab[1, n] = lower(nu, b0)
        tab[2, n] = upper(nu, b0)
        tab[3, n] = slot_node(n, b2)
        tab[4, n] = node_slot(lower(n, b3), b2)
        tab[5, n] = node_slot(upper(n, b3), b2)

    def remote(source, target, send, recv, peer):
        return pltpu.make_async_remote_copy(
            src_ref=source, dst_ref=target, send_sem=send, recv_sem=recv, device_id=peer, device_id_type=MESH
        )

    def copy1(c, s):
        return remote(s0.at[c, s], r1.at[c, s], send1.at[c, s], recv1.at[c, s], peer1)

    def copy3(c, s):
        return remote(s2.at[c, s], r3.at[c, s], send3.at[c, s], recv3.at[c, s], peer3)

    def copym(c, i):
        q = flip(near, i)
        return remote(
            pm.at[c, :, q], mid.at[c, :, near], sendm.at[c, i], recvm.at[c, i], (src, flip(tgt, i))
        )

    def copy4(c, n):
        return remote(t4.at[c, n], s4.at[c, HALF * far + n], send4.at[c, n], recv4.at[c, n], peer4)

    def copy6(c, s):
        return remote(s5.at[c, s], r6.at[c, s], send6.at[c, s], recv6.at[c, s], peer6)

    def copyg():
        return remote(g_hbm.at[4, pl.ds(HALF * (1 - far), HALF)], gpart, gs_sem, gr_sem, peer4)

    def copyo(c):
        return pltpu.make_async_copy(
            out.at[c], out_hbm.at[:, :, pl.ds(pl.multiple_of(c * WIDTH, WIDTH), WIDTH)], out_sem.at[c]
        )

    def convert(level, slot, first, second):
        for half, block in ((0, first), (1, second)):
            high = block.astype(BF16)
            gb[level, slot, :RANK, half * RANK : (half + 1) * RANK] = high
            gb[level, slot, RANK:, half * RANK : (half + 1) * RANK] = (block - high.astype(F32)).astype(BF16)

    load_g0.wait()
    for s in range(NODES):
        block = graw0[tab[0, s]]
        convert(0, s, block[:, :RANK], block[:, RANK:])
    load_x.wait()
    pl.semaphore_wait(barrier, len(peers))
    copyg().start()

    def phase_a(c, carry):
        columns = pl.ds(pl.multiple_of(c * WIDTH, WIDTH), WIDTH)
        for n in range(NODES):
            xa[n] = split(x0[n, :, columns])
        for s in range(NODES):
            (y,) = product(gb[0, s], stack(xa[tab[1, s]], xa[tab[2, s]]))
            s0[c, s] = y
            copy1(c, s).start()
        return carry

    lax.fori_loop(0, CHUNKS, phase_a, 0)

    load_g.wait()

    def convert_slot(s, carry):
        for level, row in ((2, 0), (5, 3)):
            block = graw[level - 1, tab[row, s]]
            convert(level, s, block[:, :RANK], block[:, RANK:])
        block = graw[6, s]
        convert(7, s, block[:, :RANK], block[:, RANK:])
        for level, row, side in ((1, 0, side1), (3, 0, side3), (6, 3, side6)):
            first = graw[level - 1, tab[row, s], :, pl.ds(pl.multiple_of(side * RANK, RANK), RANK)]
            second = graw[level - 1, tab[row, s], :, pl.ds(pl.multiple_of((1 - side) * RANK, RANK), RANK)]
            convert(level, s, first, second)
        return carry

    lax.fori_loop(0, NODES, convert_slot, 0)

    rows = relabel[...]
    node, row = rows >> 7, rows & 127
    position = (node_slot(node, b1) * RANK + row).astype(F32)
    lanes = lax.broadcasted_iota(jnp.int32, (RANK, RANK), 1).astype(F32)
    for q in range(NODES):
        wanted = jnp.broadcast_to(position[q : q + 1, :], (RANK, RANK)).T
        for k in range(NODES):
            onehot[q * RANK : (q + 1) * RANK, k * RANK : (k + 1) * RANK] = jnp.where(
                wanted == lanes + float(k * RANK), 1.0, 0.0
            ).astype(BF16)

    copyg().wait_recv()
    for n in range(HALF):
        block = graw[3, HALF * far + n]
        convert(4, 2 * n, block[:, :RANK], block[:, RANK:])
        block = gpart[n]
        convert(4, 2 * n + 1, block[:, :RANK], block[:, RANK:])

    def phase_b(c):
        for i in range(HALF):
            parts = []
            for s in (2 * i, 2 * i + 1):
                copy1(c, s).wait_recv()
                (y,) = product(gb[1, s], stack(split(s0[c, s]), split(r1[c, s])))
                parts.append(split(y))
            ys = product(gb[2, 2 * i : 2 * i + 2].reshape(4 * RANK, 2 * RANK), stack(*parts))
            for s, y in zip((2 * i, 2 * i + 1), ys):
                s2[c, s] = y
                copy3(c, s).start()

    def phase_c(c):
        for s in range(NODES):
            copy3(c, s).wait_recv()
            (y,) = product(gb[3, s], stack(split(s2[c, s]), split(r3[c, s])))
            xc[s * RANK : (s + 1) * RANK, :] = split(y)
        state = xc[...]
        for q in range(4):
            full = jnp.dot(onehot[q * 256 : (q + 1) * 256, :], state, preferred_element_type=F32)
            picked = full[:, :WIDTH] + full[:, WIDTH:]
            for k in range(4):
                t = 4 * q + k
                pm[c, t // 8, t % 8] = picked[k * 64 : (k + 1) * 64]
        for i in range(1, 8):
            copym(c, i).start()
        mid[c, 0, near] = pm[c, 0, near]
        mid[c, 1, near] = pm[c, 1, near]

    def phase_d(c):
        for i in range(1, 8):
            copym(c, i).wait_recv()
        for n in range(HALF):
            parts = [split(mid[c, e, 2 * n : 2 * n + 2].reshape(RANK, WIDTH)) for e in range(2)]
            own, other = product(gb[4, 2 * n : 2 * n + 2].reshape(4 * RANK, 2 * RANK), stack(*parts))
            t4[c, n] = other
            copy4(c, n).start()
            s4[c, HALF * far + n] = own

    def phase_e(c):
        for n in range(HALF):
            copy4(c, n).wait_recv()
        for n in range(NODES):
            xe[n] = split(s4[c, n])
        for i in range(HALF):
            state = stack(xe[tab[3, 2 * i]], xe[tab[3, 2 * i + 1]])
            ys = product(gb[5, 2 * i : 2 * i + 2].reshape(4 * RANK, 2 * RANK), state)
            for s, y in zip((2 * i, 2 * i + 1), ys):
                s5[c, s] = y
                copy6(c, s).start()

    def phase_f(c):
        for s in range(NODES):
            copy6(c, s).wait_recv()
            (y,) = product(gb[6, s], stack(split(s5[c, s]), split(r6[c, s])))
            xf[s] = split(y)
        for n in range(NODES):
            (y,) = product(gb[7, n], stack(xf[tab[4, n]], xf[tab[5, n]]))
            out[c, n] = y
        copyo(c).start()

    def step(k, carry):
        for delay, phase in ((0, phase_b), (1, phase_c), (4, phase_d), (5, phase_e), (6, phase_f)):

            @pl.when(jnp.logical_and(k >= delay, k < delay + CHUNKS))
            def _(delay=delay, phase=phase):
                phase(k - delay)

        return carry

    lax.fori_loop(0, CHUNKS + 6, step, 0)

    copyg().wait_send()

    def finish(c, carry):
        for s in range(NODES):
            copy1(c, s).wait_send()
            copy3(c, s).wait_send()
            copy6(c, s).wait_send()
        for i in range(1, 8):
            copym(c, i).wait_send()
        for n in range(HALF):
            copy4(c, n).wait_send()
        copyo(c).wait()
        return carry

    lax.fori_loop(0, CHUNKS, finish, 0)


def on_device(coefficients, transfer, local_bits, relabel):
    state = (CHUNKS, NODES, RANK, WIDTH)
    halves = (CHUNKS, 2, 8, 64, WIDTH)
    dma = pltpu.SemaphoreType.DMA
    return pl.pallas_call(
        kernel,
        out_shape=jax.ShapeDtypeStruct(coefficients.shape, F32),
        in_specs=[
            pl.BlockSpec(memory_space=pltpu.SMEM),
            pl.BlockSpec(memory_space=pltpu.VMEM),
            pl.BlockSpec(memory_space=pl.ANY),
            pl.BlockSpec(memory_space=pl.ANY),
        ],
        out_specs=pl.BlockSpec(memory_space=pl.ANY),
        scratch_shapes=[
            pltpu.VMEM((NODES, RANK, CHUNKS * WIDTH), F32),
            pltpu.VMEM((NODES, RANK, 2 * RANK), F32),
            pltpu.VMEM((7, NODES, RANK, 2 * RANK), F32),
            pltpu.VMEM((HALF, RANK, 2 * RANK), F32),
            pltpu.VMEM((8, NODES, 2 * RANK, 2 * RANK), BF16),
            pltpu.VMEM((NODES, RANK, 2 * WIDTH), BF16),
            pltpu.VMEM((NODES * RANK, 2 * WIDTH), BF16),
            pltpu.VMEM((NODES, RANK, 2 * WIDTH), BF16),
            pltpu.VMEM((NODES, RANK, 2 * WIDTH), BF16),
            pltpu.VMEM((NODES * RANK, NODES * RANK), BF16),
            pltpu.VMEM(state, F32),
            pltpu.VMEM(state, F32),
            pltpu.VMEM(state, F32),
            pltpu.VMEM(state, F32),
            pltpu.VMEM(halves, F32),
            pltpu.VMEM(halves, F32),
            pltpu.VMEM((CHUNKS, HALF, RANK, WIDTH), F32),
            pltpu.VMEM(state, F32),
            pltpu.VMEM(state, F32),
            pltpu.VMEM(state, F32),
            pltpu.VMEM(state, F32),
            pltpu.SMEM((6, NODES), jnp.int32),
            dma((3,)),
            dma,
            dma,
            dma((CHUNKS, NODES)),
            dma((CHUNKS, NODES)),
            dma((CHUNKS, NODES)),
            dma((CHUNKS, NODES)),
            dma((CHUNKS, NODES)),
            dma((CHUNKS, NODES)),
            dma((CHUNKS, HALF)),
            dma((CHUNKS, HALF)),
            dma((CHUNKS, NODES)),
            dma((CHUNKS, NODES)),
            dma((CHUNKS,)),
        ],
        compiler_params=pltpu.CompilerParams(
            collective_id=1, has_side_effects=True, vmem_limit_bytes=60 * 2**20
        ),
    )(local_bits, relabel.reshape(8, 128), coefficients, transfer)


def solution(mesh):
    placed = (P(("src", "tgt"), None, None), P(None, ("src", "tgt"), None, None), P(), P())
    return jax.shard_map(
        on_device,
        mesh=mesh,
        in_specs=placed,
        out_specs=P(("src", "tgt"), None, None),
        check_vma=False,
    )
```

profile of v0, /device:TPU:1, one launch (start us, length us, event | category | flops | bytes accessed | tf_op | source)
XLA Modules:
  0.0 110.4 jit_solution(5864616591292216777)
XLA Ops:
  0.0 107.3 %shard_map.46 = f32[8,128,512]{2,1,0:T(8,128)} custom-call(s32[4]{0:T(128)} %bits.1, s32[8,128]{1,0:T(8,128)} %bitcast.1, f32[8,128,512]{2,1,0:T(8,128)} %coef_hbm.1, f32[8,8,128,256]{3,2,1,0:T(8,128)} %g_hbm.1), custom_call_target="tpu_custom_call" | custom-call | tf_op jit(solution)/shard_map/pallas_call | solution.py:292
  107.3 3.1 %copy.6 = f32[8,128,512]{2,1,0:T(8,128)} copy(f32[8,128,512]{2,1,0:T(8,128)} %shard_map.46) | data formatting | bytes 4194304
where the time goes:
time: 112 us; the launch traced here: 110 us
  Pallas kernels  107 us (96%)
  local copies, waits for them, and re-layouts  3.08 us (3%)
    pallas_call x1, Pallas kernels, on_device(): pl.pallas_call(kernel, out_shape=jax.ShapeDtypeStruct(coefficients.shape,...  107 us
    unnamed x1, local copies, waits for them, and re-layouts  3.08 us

commit v1 on v0

--- a/solution.py
+++ b/solution.py
@@ -1,3 +1,5 @@
+import functools
+
 import jax
 import jax.numpy as jnp
 from jax import lax
@@ -68,13 +70,14 @@
     bits, relabel, coef_hbm, g_hbm, out_hbm,
     x0, graw0, graw, gpart, gb, xa, xc, xe, xf, onehot,
     s0, r1, s2, r3, pm, mid, t4, s4, s5, r6, out,
-    tab, in_sem, gs_sem, gr_sem,
+    tab, in_sem, x_sem, gs_sem, gr_sem,
     send1, recv1, send3, recv3, sendm, recvm, send4, recv4, send6, recv6, out_sem,
 ):
     src = lax.axis_index("src")
     tgt = lax.axis_index("tgt")
     far = lax.div(tgt, 8)
     near = tgt % 8
+    spot = [flip(lax.div(near, 2), k) for k in range(HALF)]
     peer1 = (flip(src, 8), tgt)
     peer3 = (flip(src, 1), tgt)
     peer4 = (src, flip(tgt, 8))
@@ -88,12 +91,15 @@
     for peer in peers:
         pl.semaphore_signal(barrier, inc=1, device_id=peer, device_id_type=MESH)
 
-    load_x = pltpu.make_async_copy(coef_hbm, x0, in_sem.at[0])
-    load_g0 = pltpu.make_async_copy(g_hbm.at[0], graw0, in_sem.at[1])
-    load_g = pltpu.make_async_copy(g_hbm.at[pl.ds(1, 7)], graw, in_sem.at[2])
+    def copyx(c):
+        columns = pl.ds(pl.multiple_of(c * WIDTH, WIDTH), WIDTH)
+        return pltpu.make_async_copy(coef_hbm.at[:, :, columns], x0.at[c], x_sem.at[c])
+
+    load_g0 = pltpu.make_async_copy(g_hbm.at[0], graw0, in_sem.at[0])
+    load_g = pltpu.make_async_copy(g_hbm.at[pl.ds(1, 7)], graw, in_sem.at[1])
     load_g0.start()
-    load_x.start()
-    load_g.start()
+    for c in range(CHUNKS):
+        copyx(c).start()
 
     b0, b1, b2, b3 = bits[0], bits[1], bits[2], bits[3]
     for n in range(NODES):
@@ -122,8 +128,8 @@
             pm.at[c, :, q], mid.at[c, :, near], sendm.at[c, i], recvm.at[c, i], (src, flip(tgt, i))
         )
 
-    def copy4(c, n):
-        return remote(t4.at[c, n], s4.at[c, HALF * far + n], send4.at[c, n], recv4.at[c, n], peer4)
+    def copy4(c, k):
+        return remote(t4.at[c, k], s4.at[c, HALF * far + spot[k]], send4.at[c, k], recv4.at[c, k], peer4)
 
     def copy6(c, s):
         return remote(s5.at[c, s], r6.at[c, s], send6.at[c, s], recv6.at[c, s], peer6)
@@ -146,14 +152,14 @@
     for s in range(NODES):
         block = graw0[tab[0, s]]
         convert(0, s, block[:, :RANK], block[:, RANK:])
-    load_x.wait()
+    load_g.start()
     pl.semaphore_wait(barrier, len(peers))
     copyg().start()
 
     def phase_a(c, carry):
-        columns = pl.ds(pl.multiple_of(c * WIDTH, WIDTH), WIDTH)
+        copyx(c).wait()
         for n in range(NODES):
-            xa[n] = split(x0[n, :, columns])
+            xa[n] = split(x0[c, n])
         for s in range(NODES):
             (y,) = product(gb[0, s], stack(xa[tab[1, s]], xa[tab[2, s]]))
             s0[c, s] = y
@@ -190,11 +196,11 @@
             ).astype(BF16)
 
     copyg().wait_recv()
-    for n in range(HALF):
-        block = graw[3, HALF * far + n]
-        convert(4, 2 * n, block[:, :RANK], block[:, RANK:])
-        block = gpart[n]
-        convert(4, 2 * n + 1, block[:, :RANK], block[:, RANK:])
+    for k in range(HALF):
+        block = graw[3, HALF * far + spot[k]]
+        convert(4, 2 * k, block[:, :RANK], block[:, RANK:])
+        block = gpart[spot[k]]
+        convert(4, 2 * k + 1, block[:, :RANK], block[:, RANK:])
 
     def phase_b(c):
         for i in range(HALF):
@@ -220,20 +226,21 @@
             for k in range(4):
                 t = 4 * q + k
                 pm[c, t // 8, t % 8] = picked[k * 64 : (k + 1) * 64]
-        for i in range(1, 8):
+        for i in (6, 7, 4, 5, 2, 3, 1):
             copym(c, i).start()
         mid[c, 0, near] = pm[c, 0, near]
         mid[c, 1, near] = pm[c, 1, near]
 
-    def phase_d(c):
-        for i in range(1, 8):
-            copym(c, i).wait_recv()
-        for n in range(HALF):
-            parts = [split(mid[c, e, 2 * n : 2 * n + 2].reshape(RANK, WIDTH)) for e in range(2)]
-            own, other = product(gb[4, 2 * n : 2 * n + 2].reshape(4 * RANK, 2 * RANK), stack(*parts))
-            t4[c, n] = other
-            copy4(c, n).start()
-            s4[c, HALF * far + n] = own
+    def phase_d(c, order):
+        for k in order:
+            for i in (2 * k, 2 * k + 1):
+                if i:
+                    copym(c, i).wait_recv()
+            parts = [split(mid[c, e, pl.ds(2 * spot[k], 2)].reshape(RANK, WIDTH)) for e in range(2)]
+            own, other = product(gb[4, 2 * k : 2 * k + 2].reshape(4 * RANK, 2 * RANK), stack(*parts))
+            t4[c, k] = other
+            copy4(c, k).start()
+            s4[c, HALF * far + spot[k]] = own
 
     def phase_e(c):
         for n in range(HALF):
@@ -258,7 +265,14 @@
         copyo(c).start()
 
     def step(k, carry):
-        for delay, phase in ((0, phase_b), (1, phase_c), (4, phase_d), (5, phase_e), (6, phase_f)):
+        for delay, phase in (
+            (1, phase_c),
+            (0, phase_b),
+            (4, functools.partial(phase_d, order=(3, 1))),
+            (2, functools.partial(phase_d, order=(0, 2))),
+            (5, phase_e),
+            (6, phase_f),
+        ):
 
             @pl.when(jnp.logical_and(k >= delay, k < delay + CHUNKS))
             def _(delay=delay, phase=phase):
@@ -295,12 +309,12 @@
         in_specs=[
             pl.BlockSpec(memory_space=pltpu.SMEM),
             pl.BlockSpec(memory_space=pltpu.VMEM),
-            pl.BlockSpec(memory_space=pl.ANY),
-            pl.BlockSpec(memory_space=pl.ANY),
+            pl.BlockSpec(memory_space=pltpu.HBM),
+            pl.BlockSpec(memory_space=pltpu.HBM),
         ],
         out_specs=pl.BlockSpec(memory_space=pl.ANY),
         scratch_shapes=[
-            pltpu.VMEM((NODES, RANK, CHUNKS * WIDTH), F32),
+            pltpu.VMEM(state, F32),
             pltpu.VMEM((NODES, RANK, 2 * RANK), F32),
             pltpu.VMEM((7, NODES, RANK, 2 * RANK), F32),
             pltpu.VMEM((HALF, RANK, 2 * RANK), F32),
@@ -322,7 +336,8 @@
             pltpu.VMEM(state, F32),
             pltpu.VMEM(state, F32),
             pltpu.SMEM((6, NODES), jnp.int32),
-            dma((3,)),
+            dma((2,)),
+            dma((CHUNKS,)),
             dma,
             dma,
             dma((CHUNKS, NODES)),
@@ -338,7 +353,7 @@
             dma((CHUNKS,)),
         ],
         compiler_params=pltpu.CompilerParams(
-            collective_id=1, has_side_effects=True, vmem_limit_bytes=60 * 2**20
+            collective_id=1, has_side_effects=True, vmem_limit_bytes=50 * 2**20
         ),
     )(local_bits, relabel.reshape(8, 128), coefficients, transfer)
 

time: 112 us -> 110 us (0.982)
    pallas_call x1, Pallas kernels: 107 us -> 106 us  [on_device(): pl.pallas_call(kernel, out_shape=jax.ShapeDtypeStruct(coefficients.shape,...]
    unnamed x1 -> x5, local copies, waits for them, and re-layouts: 3.08 us -> 2.66 us
where the time goes in v1:
time: 110 us; the launch traced here: 109 us
  Pallas kernels  106 us (96%)
  local copies, waits for them, and re-layouts  2.66 us (2%)
    pallas_call x1, Pallas kernels, on_device(): pl.pallas_call(kernel, out_shape=jax.ShapeDtypeStruct(coefficients.shape,...  106 us
    unnamed x5, local copies, waits for them, and re-layouts  2.66 us

profile of v1, /device:TPU:1, one launch (start us, length us, event | category | flops | bytes accessed | tf_op | source)
XLA Modules:
  0.0 108.8 jit_solution(2279481859758548164)
XLA Ops:
  0.0 0.0 copy-start
  0.0 0.7 copy-done
  0.7 0.0 copy-start.1
  0.7 0.7 copy-done.1
  1.3 106.2 %shard_map.46 = f32[8,128,512]{2,1,0:T(8,128)S(1)} custom-call(s32[4]{0:T(128)S(1)} %copy-done.1, s32[8,128]{1,0:T(8,128)S(1)} %bitcast.1, f32[8,128,512]{2,1,0:T(8,128)} %coef_hbm.1, f32[8,8,128,256]{3,2,1,0:T(8,128)} %g_hbm.1), custom_call_target="tpu_custom_call" | custom-call | tf_op jit(solution)/shard_map/pallas_call | solution.py:306
  107.5 1.3 %copy.6 = f32[8,128,512]{2,1,0:T(8,128)} copy(f32[8,128,512]{2,1,0:T(8,128)S(1)} %shard_map.46) | data formatting | bytes 4194304
Async XLA Ops:
  0.0 0.7 copy-start
  0.7 0.7 copy-start.1

commit v2 on v1

--- a/solution.py
+++ b/solution.py
@@ -202,8 +202,8 @@
         block = gpart[spot[k]]
         convert(4, 2 * k + 1, block[:, :RANK], block[:, RANK:])
 
-    def phase_b(c):
-        for i in range(HALF):
+    def phase_b(c, pairs):
+        for i in pairs:
             parts = []
             for s in (2 * i, 2 * i + 1):
                 copy1(c, s).wait_recv()
@@ -226,7 +226,7 @@
             for k in range(4):
                 t = 4 * q + k
                 pm[c, t // 8, t % 8] = picked[k * 64 : (k + 1) * 64]
-        for i in (6, 7, 4, 5, 2, 3, 1):
+        for i in (4, 5, 6, 7, 2, 3, 1):
             copym(c, i).start()
         mid[c, 0, near] = pm[c, 0, near]
         mid[c, 1, near] = pm[c, 1, near]
@@ -266,12 +266,14 @@
 
     def step(k, carry):
         for delay, phase in (
-            (1, phase_c),
-            (0, phase_b),
-            (4, functools.partial(phase_d, order=(3, 1))),
-            (2, functools.partial(phase_d, order=(0, 2))),
+            (0, functools.partial(phase_b, pairs=(0, 1))),
+            (2, functools.partial(phase_d, order=(3,))),
+            (4, functools.partial(phase_d, order=(1,))),
+            (1, functools.partial(phase_d, order=(0, 2))),
+            (0, functools.partial(phase_b, pairs=(2, 3))),
+            (0, phase_c),
+            (6, phase_f),
             (5, phase_e),
-            (6, phase_f),
         ):
 
             @pl.when(jnp.logical_and(k >= delay, k < delay + CHUNKS))

time: 110 us -> 112 us (1.018)
  Pallas kernels: 106 us -> 109 us
    pallas_call x1, Pallas kernels: 106 us -> 109 us  [on_device(): pl.pallas_call(kernel, out_shape=jax.ShapeDtypeStruct(coefficients.shape,...]
where the time goes in v2:
time: 112 us; the launch traced here: 111 us
  Pallas kernels  109 us (97%)
  local copies, waits for them, and re-layouts  2.66 us (2%)
    pallas_call x1, Pallas kernels, on_device(): pl.pallas_call(kernel, out_shape=jax.ShapeDtypeStruct(coefficients.shape,...  109 us
    unnamed x5, local copies, waits for them, and re-layouts  2.66 us

profile of v2, /device:TPU:1, one launch (start us, length us, event | category | flops | bytes accessed | tf_op | source)
XLA Modules:
  0.0 111.5 jit_solution(10839592200709228890)
XLA Ops:
  0.0 0.0 copy-start
  0.0 0.7 copy-done
  0.7 0.0 copy-start.1
  0.7 0.7 copy-done.1
  1.3 108.8 %shard_map.46 = f32[8,128,512]{2,1,0:T(8,128)S(1)} custom-call(s32[4]{0:T(128)S(1)} %copy-done.1, s32[8,128]{1,0:T(8,128)S(1)} %bitcast.1, f32[8,128,512]{2,1,0:T(8,128)} %coef_hbm.1, f32[8,8,128,256]{3,2,1,0:T(8,128)} %g_hbm.1), custom_call_target="tpu_custom_call" | custom-call | tf_op jit(solution)/shard_map/pallas_call | solution.py:308
  110.1 1.3 %copy.6 = f32[8,128,512]{2,1,0:T(8,128)} copy(f32[8,128,512]{2,1,0:T(8,128)S(1)} %shard_map.46) | data formatting | bytes 4194304
Async XLA Ops:
  0.0 0.7 copy-start
  0.7 0.7 copy-start.1

commit v3 on v1

--- a/solution.py
+++ b/solution.py
@@ -160,10 +160,11 @@
         copyx(c).wait()
         for n in range(NODES):
             xa[n] = split(x0[c, n])
-        for s in range(NODES):
-            (y,) = product(gb[0, s], stack(xa[tab[1, s]], xa[tab[2, s]]))
-            s0[c, s] = y
-            copy1(c, s).start()
+        for group in ((0, 1), (2, 3, 4), (5, 6, 7)):
+            for s in group:
+                (s0[c, s],) = product(gb[0, s], stack(xa[tab[1, s]], xa[tab[2, s]]))
+            for s in group:
+                copy1(c, s).start()
         return carry
 
     lax.fori_loop(0, CHUNKS, phase_a, 0)
@@ -207,18 +208,22 @@
             parts = []
             for s in (2 * i, 2 * i + 1):
                 copy1(c, s).wait_recv()
+            for s in (2 * i, 2 * i + 1):
                 (y,) = product(gb[1, s], stack(split(s0[c, s]), split(r1[c, s])))
                 parts.append(split(y))
             ys = product(gb[2, 2 * i : 2 * i + 2].reshape(4 * RANK, 2 * RANK), stack(*parts))
             for s, y in zip((2 * i, 2 * i + 1), ys):
                 s2[c, s] = y
+            for s in (2 * i, 2 * i + 1):
                 copy3(c, s).start()
 
     def phase_c(c):
-        for s in range(NODES):
-            copy3(c, s).wait_recv()
-            (y,) = product(gb[3, s], stack(split(s2[c, s]), split(r3[c, s])))
-            xc[s * RANK : (s + 1) * RANK, :] = split(y)
+        for group in ((0, 1, 2, 3), (4, 5, 6, 7)):
+            for s in group:
+                copy3(c, s).wait_recv()
+            for s in group:
+                (y,) = product(gb[3, s], stack(split(s2[c, s]), split(r3[c, s])))
+                xc[s * RANK : (s + 1) * RANK, :] = split(y)
         state = xc[...]
         for q in range(4):
             full = jnp.dot(onehot[q * 256 : (q + 1) * 256, :], state, preferred_element_type=F32)
@@ -236,11 +241,13 @@
             for i in (2 * k, 2 * k + 1):
                 if i:
                     copym(c, i).wait_recv()
+        for k in order:
             parts = [split(mid[c, e, pl.ds(2 * spot[k], 2)].reshape(RANK, WIDTH)) for e in range(2)]
             own, other = product(gb[4, 2 * k : 2 * k + 2].reshape(4 * RANK, 2 * RANK), stack(*parts))
             t4[c, k] = other
+            s4[c, HALF * far + spot[k]] = own
+        for k in order:
             copy4(c, k).start()
-            s4[c, HALF * far + spot[k]] = own
 
     def phase_e(c):
         for n in range(HALF):
@@ -252,11 +259,13 @@
             ys = product(gb[5, 2 * i : 2 * i + 2].reshape(4 * RANK, 2 * RANK), state)
             for s, y in zip((2 * i, 2 * i + 1), ys):
                 s5[c, s] = y
-                copy6(c, s).start()
+        for s in range(NODES):
+            copy6(c, s).start()
 
     def phase_f(c):
         for s in range(NODES):
             copy6(c, s).wait_recv()
+        for s in range(NODES):
             (y,) = product(gb[6, s], stack(split(s5[c, s]), split(r6[c, s])))
             xf[s] = split(y)
         for n in range(NODES):

time: 110 us -> 107 us (0.973)
  Pallas kernels: 106 us -> 104 us
    pallas_call x1, Pallas kernels: 106 us -> 104 us  [on_device(): pl.pallas_call(kernel, out_shape=jax.ShapeDtypeStruct(coefficients.shape,...]
where the time goes in v3:
time: 107 us; the launch traced here: 106 us
  Pallas kernels  104 us (97%)
  local copies, waits for them, and re-layouts  2.66 us (2%)
    pallas_call x1, Pallas kernels, on_device(): pl.pallas_call(kernel, out_shape=jax.ShapeDtypeStruct(coefficients.shape,...  104 us
    unnamed x5, local copies, waits for them, and re-layouts  2.66 us

profile of v3, /device:TPU:1, one launch (start us, length us, event | category | flops | bytes accessed | tf_op | source)
XLA Modules:
  0.0 106.4 jit_solution(7109269529607702263)
XLA Ops:
  0.0 0.0 copy-start
  0.0 0.7 copy-done
  0.7 0.0 copy-start.1
  0.7 0.7 copy-done.1
  1.3 103.7 %shard_map.46 = f32[8,128,512]{2,1,0:T(8,128)S(1)} custom-call(s32[4]{0:T(128)S(1)} %copy-done.1, s32[8,128]{1,0:T(8,128)S(1)} %bitcast.1, f32[8,128,512]{2,1,0:T(8,128)} %coef_hbm.1, f32[8,8,128,256]{3,2,1,0:T(8,128)} %g_hbm.1), custom_call_target="tpu_custom_call" | custom-call | tf_op jit(solution)/shard_map/pallas_call | solution.py:315
  105.1 1.3 %copy.6 = f32[8,128,512]{2,1,0:T(8,128)} copy(f32[8,128,512]{2,1,0:T(8,128)S(1)} %shard_map.46) | data formatting | bytes 4194304
Async XLA Ops:
  0.0 0.7 copy-start
  0.7 0.7 copy-start.1

commit v4 on v3

--- a/solution.py
+++ b/solution.py
@@ -203,8 +203,8 @@
         block = gpart[spot[k]]
         convert(4, 2 * k + 1, block[:, :RANK], block[:, RANK:])
 
-    def phase_b(c):
-        for i in range(HALF):
+    def phase_b(c, pairs):
+        for i in pairs:
             parts = []
             for s in (2 * i, 2 * i + 1):
                 copy1(c, s).wait_recv()
@@ -231,7 +231,7 @@
             for k in range(4):
                 t = 4 * q + k
                 pm[c, t // 8, t % 8] = picked[k * 64 : (k + 1) * 64]
-        for i in (6, 7, 4, 5, 2, 3, 1):
+        for i in (4, 5, 6, 7, 2, 3, 1):
             copym(c, i).start()
         mid[c, 0, near] = pm[c, 0, near]
         mid[c, 1, near] = pm[c, 1, near]
@@ -274,16 +274,21 @@
         copyo(c).start()
 
     def step(k, carry):
-        for delay, phase in (
-            (1, phase_c),
-            (0, phase_b),
-            (4, functools.partial(phase_d, order=(3, 1))),
-            (2, functools.partial(phase_d, order=(0, 2))),
-            (5, phase_e),
-            (6, phase_f),
+        early = functools.partial(phase_d, order=(0, 2))
+        late = functools.partial(phase_d, order=(3, 1))
+        for delay, first, last, phase in (
+            (1, 0, 3, phase_c),
+            (2, 0, 1, early),
+            (0, 0, 3, functools.partial(phase_b, pairs=(0, 1))),
+            (1, 2, 2, early),
+            (0, 0, 3, functools.partial(phase_b, pairs=(2, 3))),
+            (4, 0, 3, late),
+            (2, 3, 3, early),
+            (5, 0, 3, phase_e),
+            (6, 0, 3, phase_f),
         ):
 
-            @pl.when(jnp.logical_and(k >= delay, k < delay + CHUNKS))
+            @pl.when(jnp.logical_and(k >= delay + first, k <= delay + last))
             def _(delay=delay, phase=phase):
                 phase(k - delay)
 

time: 107 us -> 106 us (level)
  no operation moved by 1% of the time
where the time goes in v4:
time: 106 us
  Pallas kernels  103 us (97%)
  local copies, waits for them, and re-layouts  2.66 us (3%)
    pallas_call x1, Pallas kernels, on_device(): pl.pallas_call(kernel, out_shape=jax.ShapeDtypeStruct(coefficients.shape,...  103 us
    unnamed x5, local copies, waits for them, and re-layouts  2.66 us

profile of v4, /device:TPU:1, one launch (start us, length us, event | category | flops | bytes accessed | tf_op | source)
XLA Modules:
  0.0 105.8 jit_solution(15431067797335745231)
XLA Ops:
  0.0 0.0 copy-start
  0.0 0.7 copy-done
  0.7 0.0 copy-start.1
  0.7 0.7 copy-done.1
  1.3 103.1 %shard_map.46 = f32[8,128,512]{2,1,0:T(8,128)S(1)} custom-call(s32[4]{0:T(128)S(1)} %copy-done.1, s32[8,128]{1,0:T(8,128)S(1)} %bitcast.1, f32[8,128,512]{2,1,0:T(8,128)} %coef_hbm.1, f32[8,8,128,256]{3,2,1,0:T(8,128)} %g_hbm.1), custom_call_target="tpu_custom_call" | custom-call | tf_op jit(solution)/shard_map/pallas_call | solution.py:320
  104.5 1.3 %copy.6 = f32[8,128,512]{2,1,0:T(8,128)} copy(f32[8,128,512]{2,1,0:T(8,128)S(1)} %shard_map.46) | data formatting | bytes 4194304
Async XLA Ops:
  0.0 0.7 copy-start
  0.7 0.7 copy-start.1

commit v5 on v4

--- a/solution.py
+++ b/solution.py
@@ -137,10 +137,10 @@
     def copyg():
         return remote(g_hbm.at[4, pl.ds(HALF * (1 - far), HALF)], gpart, gs_sem, gr_sem, peer4)
 
-    def copyo(c):
-        return pltpu.make_async_copy(
-            out.at[c], out_hbm.at[:, :, pl.ds(pl.multiple_of(c * WIDTH, WIDTH), WIDTH)], out_sem.at[c]
-        )
+    def copyo(c, h):
+        columns = pl.ds(pl.multiple_of(c * WIDTH, WIDTH), WIDTH)
+        nodes = pl.ds(h * HALF, HALF)
+        return pltpu.make_async_copy(out.at[c, nodes], out_hbm.at[nodes, :, columns], out_sem.at[c, h])
 
     def convert(level, slot, first, second):
         for half, block in ((0, first), (1, second)):
@@ -153,8 +153,6 @@
         block = graw0[tab[0, s]]
         convert(0, s, block[:, :RANK], block[:, RANK:])
     load_g.start()
-    pl.semaphore_wait(barrier, len(peers))
-    copyg().start()
 
     def phase_a(c, carry):
         copyx(c).wait()
@@ -163,6 +161,13 @@
         for group in ((0, 1), (2, 3, 4), (5, 6, 7)):
             for s in group:
                 (s0[c, s],) = product(gb[0, s], stack(xa[tab[1, s]], xa[tab[2, s]]))
+            if group[0] == 0:
+
+                @pl.when(c == 0)
+                def _():
+                    pl.semaphore_wait(barrier, len(peers))
+                    copyg().start()
+
             for s in group:
                 copy1(c, s).start()
         return carry
@@ -271,7 +276,8 @@
         for n in range(NODES):
             (y,) = product(gb[7, n], stack(xf[tab[4, n]], xf[tab[5, n]]))
             out[c, n] = y
-        copyo(c).start()
+            if n % HALF == HALF - 1:
+                copyo(c, n // HALF).start()
 
     def step(k, carry):
         early = functools.partial(phase_d, order=(0, 2))
@@ -307,7 +313,8 @@
             copym(c, i).wait_send()
         for n in range(HALF):
             copy4(c, n).wait_send()
-        copyo(c).wait()
+        for h in range(2):
+            copyo(c, h).wait()
         return carry
 
     lax.fori_loop(0, CHUNKS, finish, 0)
@@ -364,7 +371,7 @@
             dma((CHUNKS, HALF)),
             dma((CHUNKS, NODES)),
             dma((CHUNKS, NODES)),
-            dma((CHUNKS,)),
+            dma((CHUNKS, 2)),
         ],
         compiler_params=pltpu.CompilerParams(
             collective_id=1, has_side_effects=True, vmem_limit_bytes=50 * 2**20

time: 106 us -> 106 us (level)
  no operation moved by 1% of the time
where the time goes in v5:
time: 106 us
  Pallas kernels  103 us (97%)
  local copies, waits for them, and re-layouts  2.66 us (3%)
    pallas_call x1, Pallas kernels, on_device(): pl.pallas_call(kernel, out_shape=jax.ShapeDtypeStruct(coefficients.shape,...  103 us
    unnamed x5, local copies, waits for them, and re-layouts  2.66 us

profile of v5, /device:TPU:1, one launch (start us, length us, event | category | flops | bytes accessed | tf_op | source)
XLA Modules:
  0.0 106.1 jit_solution(13250536854537988439)
XLA Ops:
  0.0 0.0 copy-start
  0.0 0.7 copy-done
  0.7 0.0 copy-start.1
  0.7 0.7 copy-done.1
  1.3 103.4 %shard_map.46 = f32[8,128,512]{2,1,0:T(8,128)S(1)} custom-call(s32[4]{0:T(128)S(1)} %copy-done.1, s32[8,128]{1,0:T(8,128)S(1)} %bitcast.1, f32[8,128,512]{2,1,0:T(8,128)} %coef_hbm.1, f32[8,8,128,256]{3,2,1,0:T(8,128)} %g_hbm.1), custom_call_target="tpu_custom_call" | custom-call | tf_op jit(solution)/shard_map/pallas_call | solution.py:327
  104.8 1.3 %copy.6 = f32[8,128,512]{2,1,0:T(8,128)} copy(f32[8,128,512]{2,1,0:T(8,128)S(1)} %shard_map.46) | data formatting | bytes 4194304
Async XLA Ops:
  0.0 0.7 copy-start
  0.7 0.7 copy-start.1
